TPU v7x, 256 devices: a whole 4x4x8 slice. The times are simulated.
256 devices in a mesh: dp: 32 (over y, x, core), ctx: 8 (over z).
Axes of the slice: x: 4, y: 4, z: 8, core: 2. Of those that a mesh axis runs over, the one named last changes fastest.
Arguments:
- value: bfloat16 [32, 1024, 512], P('dp', 'ctx'), may hold values from -6 to 6
- gate_one: bfloat16 [32, 1024, 512], P('dp', 'ctx'), may hold values from -6 to 6
- gate_two: bfloat16 [32, 1024, 512], P('dp', 'ctx'), may hold values from -6 to 6
- filters: bfloat16 [2, 1024, 512], replicated, may hold values from -0.1875 to 0.1875
- out_weight: bfloat16 [512, 512], replicated, may hold values from -0.25 to 0.25
- grad_out: bfloat16 [32, 1024, 512], P('dp', 'ctx'), may hold values from -6 to 6
Outputs:
- mixed: bfloat16 [32, 1024, 512], P('dp', 'ctx')
- grad_value: bfloat16 [32, 1024, 512], P('dp', 'ctx')
- grad_gate_one: bfloat16 [32, 1024, 512], P('dp', 'ctx')
- grad_gate_two: bfloat16 [32, 1024, 512], P('dp', 'ctx')
- filter_grad: float32 [2, 1024, 512], P(None, 'ctx', 'dp')
- weight_grad: float32 [512, 512], P('dp', 'ctx')
All inputs are finite; a program needn't handle non-finite values.
Results may differ from a plain program's by a relative error of at most 0.019.
Values may be sent and summed in bfloat16 or wider, within the bound.
A program may use at most 128 MiB of HBM per device.

v0:
```python
import math
import jax
import jax.numpy as jnp
from jax import lax
from jax.sharding import PartitionSpec as P


def make_tables(block):
    period = 2 * block
    freq_bins = jnp.concatenate(
        [jnp.arange(block + 1, dtype=jnp.int32), jnp.arange(1, block, dtype=jnp.int32)]
    )
    sine_rows = jnp.arange(period, dtype=jnp.int32) > block
    inputs = jnp.arange(block, dtype=jnp.int32)
    turns = freq_bins[:, None] * inputs[None, :] % period
    radians = turns.astype(jnp.float32) * (2.0 * math.pi / period)
    forward = jnp.where(sine_rows[:, None], jnp.sin(radians), jnp.cos(radians))
    moments = jnp.arange(period, dtype=jnp.int32)
    turns_back = moments[:, None] * freq_bins[None, :] % period
    radians_back = turns_back.astype(jnp.float32) * (2.0 * math.pi / period)
    border_bins = (freq_bins == 0) | (freq_bins == block)
    weights = jnp.where(border_bins, 1.0, 2.0) / period
    inverse = (
        jnp.where(sine_rows[None, :], jnp.sin(radians_back), jnp.cos(radians_back))
        * weights[None, :]
    )
    parity = jnp.where(freq_bins % 2 == 0, 1.0, -1.0).astype(jnp.float32)[:, None]
    return (forward, inverse, parity)


def to_spectra(blocks, table):
    return jnp.einsum(
        "fb,...bd->...fd", table, blocks.astype(jnp.float32), precision=lax.Precision.HIGHEST
    )


def from_spectra(table, spectra):
    return jnp.einsum("tf,...fd->...td", table, spectra, precision=lax.Precision.HIGHEST)


def spectral_product(left, right, block, conj_left):
    left_real = left[..., : block + 1, :]
    left_imag = left[..., block + 1 :, :]
    right_real = right[..., : block + 1, :]
    right_imag = right[..., block + 1 :, :]
    if conj_left:
        left_imag = -left_imag
    cross = left_imag * right_imag
    border = jnp.zeros_like(cross[..., :1, :])
    real_part = left_real * right_real - jnp.concatenate([border, cross, border], axis=-2)
    imag_part = left_real[..., 1:block, :] * right_imag + left_imag * right_real[..., 1:block, :]
    return jnp.concatenate([real_part, imag_part], axis=-2)


def on_device(value, gate_one, gate_two, filters, out_weight, grad_out):
    rows = value.shape[1]
    width = value.shape[2]
    seq_count = lax.axis_size("ctx")
    data_count = lax.axis_size("dp")
    position = lax.axis_index("ctx")
    block = math.gcd(rows, 128)
    own_blocks = rows // block
    lag_blocks = own_blocks * seq_count
    forward, inverse, parity = make_tables(block)
    low_rows = inverse[:block]
    high_rows = inverse[block:]
    first_block = position * own_blocks
    own_start = position * rows
    filter_blocks = filters.reshape(2, lag_blocks, block, width)
    filter_spectra = to_spectra(filter_blocks, forward)
    padded_filters = jnp.concatenate([jnp.zeros_like(filter_spectra), filter_spectra], axis=1)

    def piece_spectra_of(piece):
        count = piece.shape[0] // block
        return to_spectra(piece.reshape(count, block, width), forward)

    def causal(source, padded_filter):
        initial = jnp.zeros((own_blocks + 1, 2 * block, width), jnp.float32)
        piece = lax.all_gather(source, "ctx", axis=0, tiled=True)
        start = jnp.int32(0)

        def work(total):
            piece_spectra = piece_spectra_of(piece)
            count = piece_spectra.shape[0]
            start_block = start // block
            last_block = start_block + count - 1
            terms_list = []
            for index in range(own_blocks + 1):
                out_block = first_block - 1 + index
                anchor = jnp.maximum(out_block, 0)
                window = lax.dynamic_slice_in_dim(
                    padded_filter, lag_blocks + anchor - last_block, count, 0
                )
                window = jnp.flip(window, 0)
                summed_term = jnp.sum(spectral_product(window, piece_spectra, block, False), axis=0)
                if index == 0:
                    summed_term = summed_term * (out_block >= 0).astype(jnp.float32)
                terms_list.append(summed_term)
            return total + jnp.stack(terms_list)

        summed = lax.cond(start < own_start + rows, work, lambda total: total, initial)
        lower = from_spectra(low_rows, summed[1:])
        upper = from_spectra(high_rows, summed[:-1])
        return (lower + upper).reshape(rows, width)

    def anti_owner(source, grad_rows, padded_filter):
        filter_spectrum = padded_filter[lag_blocks:]
        whole_source, whole_grad = (
            lax.all_gather(source, "ctx", axis=0, tiled=True),
            lax.all_gather(grad_rows, "ctx", axis=0, tiled=True),
        )
        source_spectra = piece_spectra_of(whole_source)
        grad_spectra = piece_spectra_of(whole_grad)
        following = (
            jnp.concatenate([grad_spectra[1:], jnp.zeros_like(grad_spectra[:1])], axis=0) * parity
        )
        combined = grad_spectra + following
        padded = jnp.concatenate([combined, jnp.zeros_like(combined)], axis=0)

        def one_block(offset):
            window = lax.dynamic_slice_in_dim(padded, offset, lag_blocks, 0)
            grad_piece = jnp.sum(spectral_product(filter_spectrum, window, block, True), axis=0)
            lag_piece = jnp.sum(spectral_product(source_spectra, window, block, True), axis=0)
            return (grad_piece, lag_piece)

        grad_parts, lag_parts = lax.map(
            one_block, first_block + jnp.arange(own_blocks, dtype=jnp.int32)
        )
        grad_part = from_spectra(low_rows, grad_parts).reshape(rows, width)
        lag_part = from_spectra(low_rows, lag_parts).reshape(rows, width)
        return (grad_part, lag_part)

    def backward(source, grad_rows, padded_filter):
        return anti_owner(source, grad_rows, padded_filter)

    value_rows = value[0]
    gate_first = gate_one[0].astype(jnp.float32)
    gate_second = gate_two[0].astype(jnp.float32)
    cotangent = grad_out[0]
    first_conv = causal(value_rows, padded_filters[0])
    mixed_input = (gate_first * first_conv).astype(jnp.bfloat16)
    second_conv = causal(mixed_input, padded_filters[1])
    gated = (gate_second * second_conv).astype(jnp.bfloat16)
    mixed = jnp.dot(gated, out_weight, preferred_element_type=jnp.float32).astype(jnp.bfloat16)
    grad_gated = lax.dot_general(
        cotangent, out_weight, (((1,), (1,)), ((), ())), preferred_element_type=jnp.float32
    )
    grad_gate_two = (grad_gated * second_conv).astype(jnp.bfloat16)
    grad_second = (grad_gated * gate_second).astype(jnp.bfloat16)
    grad_mixed, lag_second = backward(mixed_input, grad_second, padded_filters[1])
    grad_gate_one = (grad_mixed * first_conv).astype(jnp.bfloat16)
    grad_first = (grad_mixed * gate_first).astype(jnp.bfloat16)
    grad_value_full, lag_first = backward(value_rows, grad_first, padded_filters[0])
    grad_value = grad_value_full.astype(jnp.bfloat16)
    own_lags = jnp.stack([lag_first, lag_second])
    filter_grad = (
        lax.psum_scatter(
            own_lags.astype(jnp.bfloat16), "dp", scatter_dimension=2, tiled=True
        ).astype(jnp.float32)
        / data_count
    )
    weight_part = lax.psum_scatter(
        lax.dot_general(
            gated, cotangent, (((0,), (0,)), ((), ())), preferred_element_type=jnp.float32
        ).astype(jnp.bfloat16),
        "dp",
        scatter_dimension=0,
        tiled=True,
    )
    weight_grad = (
        lax.psum_scatter(weight_part, "ctx", scatter_dimension=1, tiled=True).astype(jnp.float32)
        / data_count
    )
    return (
        mixed[None],
        grad_value[None],
        grad_gate_one[None],
        grad_gate_two[None],
        filter_grad,
        weight_grad,
    )


def solution(mesh):
    return jax.shard_map(
        on_device,
        mesh=mesh,
        in_specs=(
            P("dp", "ctx", None),
            P("dp", "ctx", None),
            P("dp", "ctx", None),
            P(),
            P(),
            P("dp", "ctx", None),
        ),
        out_specs=(
            P("dp", "ctx", None),
            P("dp", "ctx", None),
            P("dp", "ctx", None),
            P("dp", "ctx", None),
            P(None, "ctx", "dp"),
            P("dp", "ctx"),
        ),
        check_vma=False,
    )
```

profile of v0, /device:TPU:2, one launch (start us, length us, event | category | flops | bytes accessed | tf_op | source)
XLA Modules:
  0.0 464.7 jit_solution(18322438985190754017)
XLA Ops:
  9.2 3.9 convolution_bitcast_fusion.2
  13.1 8.0 %concatenate.92 = f32[2,16,256,512]{3,2,1,0:T(8,128)} pad(f32[2,8,256,512]{3,2,1,0:T(8,128)S(1)} %convolution_bitcast_fusion.2, f32[]{:T(128)} %constant.162.clone.1), padding=0_0x8_0x0_0x0_0 | pad | bytes 25165828 | tf_op jit(solution)/shard_map/concatenate | solution.py:71
  23.7 27.5 %all-gather.10.cloned.1.call-done = bf16[1,1024,512]{2,1,0:T(8,128)(2,1)} async-done(((bf16[1,128,512]{2,1,0:T(8,128)(2,1)}), bf16[1,1024,512]{2,1,0:T(8,128)(2,1)}) %all-gather.10.cloned.1.call-update) | async-done | bytes 1048592 | tf_op jit(solution)/shard_map/all_gather | solution.py:79
  51.2 27.0 %conditional.2 = (f32[2,256,512]{2,1,0:T(8,128)S(1)}) conditional(s32[]{:T(128)} %convert_element_type.91, () %tuple.25, (f32[2,16,256,512]{3,2,1,0:T(8,128)}, s32[]{:T(128)}, bf16[1024,512]{1,0:T(8,128)(2,1)}, f32[256,128]{1,0:T(8,128)}) %tuple.88), branch_computations={%region_0.1_spmd, %region_1.4_spmd} | conditional | flops 1623326720 | bytes 141476128 | solution.py:101
  51.2 4.4 slice.174
  58.8 3.8 fusion.87
  62.6 3.1 convolution_bitcast_fusion
  65.8 7.3 %reverse_multiply_fusion.1 = (f32[8,127,512]{2,1,0:T(8,128)}, f32[8,127,512]{2,1,0:T(8,128)S(1)}, f32[8,127,512]{2,1,0:T(8,128)}, f32[8,127,512]{2,1,0:T(8,128)}) fusion(f32[8,127,512]{2,1,0:T(8,128)S(1)} %copy-done.12, f32[8,256,512]{2,1,0:T(8,128)S(1)} %convolution_bitcast_fusion, f32[8,127,512]{2,1,0:T(8,128)} %get-tuple-element.115, ...), kind=kLoop, calls=%fused_computation.14 | loop fusion | flops 4161536 | bytes 20807680 | tf_op jit(solution)/shard_map/cond/branch_1_fun/mul | solution.py:48
  73.1 3.8 fusion
  81.5 37.6 %all-gather.12.cloned.1.call-done = bf16[1,1024,512]{1,2,0:T(8,128)(2,1)} async-done(((bf16[1,128,512]{1,2,0:T(8,128)(2,1)}), bf16[1,1024,512]{1,2,0:T(8,128)(2,1)}) %all-gather.12.cloned.1.call-update) | async-done | bytes 1048592 | tf_op jit(solution)/shard_map/all_gather | solution.py:79
  119.2 32.5 %conditional.3 = (f32[2,256,512]{2,1,0:T(8,128)S(1)}) conditional(s32[]{:T(128)} %convert_element_type.91, () %tuple.24, (f32[2,16,256,512]{3,2,1,0:T(8,128)}, s32[]{:T(128)}, bf16[1024,512]{0,1:T(8,128)(2,1)}, f32[256,128]{1,0:T(8,128)}) %tuple.87), branch_computations={%region_4.5_spmd, %region_5.8_spmd} | conditional | flops 1623326720 | bytes 147833088 | solution.py:101
  120.7 2.9 convolution_bitcast_fusion.1
  123.6 4.4 slice.190
  128.0 3.1 dynamic-slice_bitcast_fusion.3
  134.9 3.8 fusion.89
  138.7 7.9 %reverse_multiply_fusion.3 = (f32[8,127,512]{2,1,0:T(8,128)}, f32[8,127,512]{2,1,0:T(8,128)S(1)}, f32[8,127,512]{2,1,0:T(8,128)}, f32[8,127,512]{2,1,0:T(8,128)}) fusion(f32[8,127,512]{2,1,0:T(8,128)} %get-tuple-element.130, f32[8,256,512]{2,1,0:T(8,128)S(1)} %convolution_bitcast_fusion.1, f32[8,127,512]{2,1,0:T(8,128)} %get-tuple-element.131, ...), kind=kLoop, calls=%fused_computation.32 | loop fusion | flops 4161536 | bytes 20807680 | tf_op jit(solution)/shard_map/cond/branch_1_fun/mul | solution.py:48
  146.6 3.8 fusion.3
  157.1 8.2 %slice_bitcast_fusion = (f32[8,256,512]{2,1,0:T(8,128)}, f32[8,256,512]{2,1,0:T(8,128)}) fusion(f32[2,8,256,512]{3,2,1,0:T(8,128)} %copy-done.2), kind=kLoop, calls=%fused_computation.50 | loop fusion | bytes 16777216 | tf_op jit(solution)/shard_map/slice | solution.py:107
  165.9 4.5 convolution_bitcast_fusion.3
  170.4 69.5 %reduce-scatter.8.cloned.1.call-done = bf16[16,512]{1,0:T(8,128)(2,1)} async-done(((bf16[512,512]{1,0:T(8,128)(2,1)}), bf16[16,512]{1,0:T(8,128)(2,1)}) %reduce-scatter.8.cloned.1.call-update) | async-done | bytes 16400 | tf_op jit(solution)/shard_map/reduce_scatter | solution.py:162
  241.5 39.6 %all-gather.8.cloned.1.call-done = bf16[1024,512]{0,1:T(8,128)(2,1)} async-done(((bf16[128,512]{0,1:T(8,128)(2,1)}), bf16[1024,512]{0,1:T(8,128)(2,1)}) %all-gather.8.cloned.1.call-update) | async-done | bytes 1048592 | tf_op jit(solution)/shard_map/all_gather | solution.py:110
  289.3 3.8 fusion.17
  293.1 3.7 fusion.9
  296.8 3.8 maximum_reduce_fusion.4
  302.6 5.1 %convolution_bitcast_fusion.4 = f32[8,256,512]{2,1,0:T(8,128)} fusion(bf16[8,128,512]{2,1,0:T(8,128)(2,1)S(1)} %bitcast.158, s32[256]{0:T(256)} %copy-done.28, pred[256]{0:T(512)(128)(4,1)} %copy-done.30), kind=kOutput, calls=%fused_computation.68 | convolution fusion | flops 1611104256 | bytes 5244160 | tf_op jit(solution)/shard_map/fb,...bd->...fd/dot_general | solution.py:32
  309.4 10.1 %reduce-scatter.10.cloned.1.call-done = bf16[64,16]{1,0:T(8,128)(2,1)} async-done(((bf16[512,16]{1,0:T(8,128)(2,1)}), bf16[64,16]{1,0:T(8,128)(2,1)}) %reduce-scatter.10.cloned.1.call-update) | async-done | bytes 2064
  321.3 38.3 %all-gather.14.cloned.1.call-done = bf16[1,1024,512]{1,2,0:T(8,128)(2,1)} async-done(((bf16[1,128,512]{1,2,0:T(8,128)(2,1)}), bf16[1,1024,512]{1,2,0:T(8,128)(2,1)}) %all-gather.14.cloned.1.call-update) | async-done | bytes 1048592 | tf_op jit(solution)/shard_map/all_gather | solution.py:110
  361.1 2.6 convolution_bitcast_fusion.5
  367.9 3.1 fusion.16
  370.9 4.4 fusion.8
  379.1 3.0 maximum_reduce_fusion.5
  383.8 72.5 %reduce-scatter.6.cloned.1.call-done = bf16[2,128,16]{1,2,0:T(8,128)(2,1)} async-done(((bf16[2,128,512]{1,2,0:T(8,128)(2,1)}), bf16[2,128,16]{1,2,0:T(8,128)(2,1)}) %reduce-scatter.6.cloned.1.call-update) | async-done | bytes 8208 | tf_op jit(solution)/shard_map/reduce_scatter | solution.py:157
  (136 shorter events, 52.3 us)
Async XLA Ops:
  7.2 44.0 %all-gather.10.cloned.1.call-start = ((), (), s32[]{:S(2)}) async-start(), calls=%async_computation.6 | async-start | bytes 1179648 | tf_op jit(solution)/shard_map/all_gather | solution.py:79
  7.9 111.3 %all-gather.12.cloned.1.call-start = ((), (), s32[]{:S(2)}) async-start(), calls=%async_computation.7 | async-start | bytes 1179648 | tf_op jit(solution)/shard_map/all_gather | solution.py:79
  9.0 70.6 %copy-start.21 = (bf16[1,128,512]{1,2,0:T(8,128)(2,1)}, bf16[1,128,512]{1,2,0:T(8,128)(2,1)S(1)}, u32[]{:S(2)}) copy-start(bf16[1,128,512]{1,2,0:T(8,128)(2,1)S(1)} %copy.24) | copy-start | bytes 393220
  9.0 273.6 %copy-start.30 = (pred[256]{0:T(512)(128)(4,1)}, pred[256]{0:T(512)(128)(4,1)S(1)}, u32[]{:S(2)}) copy-start(pred[256]{0:T(512)(128)(4,1)S(1)} %iota_compare_fusion) | copy-start | bytes 772
  9.1 273.5 %copy-start.28 = (s32[256]{0:T(256)}, s32[256]{0:T(256)S(1)}, u32[]{:S(2)}) copy-start(s32[256]{0:T(256)S(1)} %get-tuple-element.103) | copy-start | bytes 3076
  9.1 276.7 %copy-start.32 = (f32[256]{0:T(256)}, f32[256]{0:T(256)S(1)}, u32[]{:S(2)}) copy-start(f32[256]{0:T(256)S(1)} %get-tuple-element.102) | copy-start | bytes 3076
  13.1 8.3 %copy-start.2 = (f32[2,8,256,512]{3,2,1,0:T(8,128)}, f32[2,8,256,512]{3,2,1,0:T(8,128)S(1)}, u32[]{:S(2)}) copy-start(f32[2,8,256,512]{3,2,1,0:T(8,128)S(1)} %convolution_bitcast_fusion.2) | copy-start | bytes 25165828
  58.8 3.8 copy-start.17
  65.8 7.3 %copy-start.8 = (f32[8,129,512]{2,1,0:T(8,128)S(1)}, f32[8,129,512]{2,1,0:T(8,128)}, u32[]{:S(2)}) copy-start(f32[8,129,512]{2,1,0:T(8,128)} %slice.272) | copy-start | bytes 6340612 | tf_op jit(solution)/shard_map/cond
  73.1 3.8 copy-start.10
  81.3 158.6 %reduce-scatter.8.cloned.1.call-start = ((), (), s32[]{:S(2)}) async-start(), calls=%async_computation.5 | async-start | bytes 540672 | tf_op jit(solution)/shard_map/reduce_scatter | solution.py:162
  138.7 7.9 %copy-start.9 = (f32[8,129,512]{2,1,0:T(8,128)S(1)}, f32[8,129,512]{2,1,0:T(8,128)}, u32[]{:S(2)}) copy-start(f32[8,129,512]{2,1,0:T(8,128)} %slice.281) | copy-start | bytes 6340612 | tf_op jit(solution)/shard_map/cond
  146.6 3.8 copy-start.11
  151.7 4.4 copy-start.19
  151.7 4.4 copy-start.26
  156.0 125.1 %all-gather.8.cloned.1.call-start = ((), (), s32[]{:S(2)}) async-start(), calls=%async_computation.3 | async-start | bytes 1179648 | tf_op jit(solution)/shard_map/all_gather | solution.py:110
  157.1 162.4 %reduce-scatter.10.cloned.1.call-start = ((), (), s32[]{:S(2)}) async-start(), calls=%async_computation.9 | async-start | bytes 147456
  157.1 8.2 %copy-start.13 = (bf16[1,1024,512]{1,2,0:T(8,128)(2,1)S(1)}, bf16[1,1024,512]{1,2,0:T(8,128)(2,1)}, u32[]{:S(2)}) copy-start(bf16[1,1024,512]{1,2,0:T(8,128)(2,1)} %all-gather.12.cloned.1.call-done) | copy-start | bytes 3145732
  241.4 118.1 %all-gather.14.cloned.1.call-start = ((), (), s32[]{:S(2)}) async-start(), calls=%async_computation.8 | async-start | bytes 1179648 | tf_op jit(solution)/shard_map/all_gather | solution.py:110
  285.8 3.5 copy-start.6
  296.8 3.8 copy-start.22
  296.8 3.8 copy-start.23
  296.8 5.8 %copy-start.16 = (bf16[1,1024,512]{2,1,0:T(8,128)(2,1)S(1)}, bf16[1,1024,512]{2,1,0:T(8,128)(2,1)}, u32[]{:S(2)}) copy-start(bf16[1,1024,512]{2,1,0:T(8,128)(2,1)} %all-gather.10.cloned.1.call-done) | copy-start | bytes 3145732
  302.3 154.0 %reduce-scatter.6.cloned.1.call-start = ((), (), s32[]{:S(2)}) async-start(), calls=%async_computation.4 | async-start | bytes 270336 | tf_op jit(solution)/shard_map/reduce_scatter | solution.py:157
  302.5 5.2 %copy-start.24 = (bf16[1,128,512]{1,2,0:T(8,128)(2,1)S(1)}, bf16[1,128,512]{1,2,0:T(8,128)(2,1)}, u32[]{:S(2)}) copy-start(bf16[1,128,512]{1,2,0:T(8,128)(2,1)} %get-tuple-element.154) | copy-start | bytes 393220
  302.6 6.0 %copy-start.15 = (f32[512,128]{1,0:T(8,128)S(1)}, f32[512,128]{1,0:T(8,128)}, u32[]{:S(2)}) copy-start(f32[512,128]{1,0:T(8,128)} %copy-done.14) | copy-start | bytes 786436
  302.6 6.0 %copy-start.20 = (bf16[512,512]{1,0:T(8,128)(2,1)S(1)}, bf16[512,512]{1,0:T(8,128)(2,1)}, u32[]{:S(2)}) copy-start(bf16[512,512]{1,0:T(8,128)(2,1)} %param.14) | copy-start | bytes 1572868
  302.6 17.7 %copy-start.18 = (f32[256,512]{1,0:T(8,128)S(1)}, f32[256,512]{1,0:T(8,128)}, u32[]{:S(2)}) copy-start(f32[256,512]{1,0:T(8,128)} %get-tuple-element.161) | copy-start | bytes 1572868
  307.7 53.3 %copy-start.29 = (s32[256]{0:T(256)S(1)}, s32[256]{0:T(256)}, u32[]{:S(2)}) copy-start(s32[256]{0:T(256)} %copy-done.28) | copy-start | bytes 3076
  307.7 53.3 %copy-start.31 = (pred[256]{0:T(512)(128)(4,1)S(1)}, pred[256]{0:T(512)(128)(4,1)}, u32[]{:S(2)}) copy-start(pred[256]{0:T(512)(128)(4,1)} %copy-done.30) | copy-start | bytes 772
  364.4 3.5 copy-start.5
  379.1 78.6 %copy-start.1 = (bf16[2,1024,512]{2,1,0:T(8,128)(2,1)S(1)}, bf16[2,1024,512]{2,1,0:T(8,128)(2,1)}, u32[]{:S(2)}) copy-start(bf16[2,1024,512]{2,1,0:T(8,128)(2,1)} %param.13) | copy-start | bytes 6291460
  (9 other events, 21.8 us)
Sparse Core Ops, SparseCore 0:
  9.8 41.3 all-gather.9
  81.5 37.6 all-gather.11
  156.1 83.7 reduce-scatter.7
  242.1 38.9 all-gather.7
  283.4 36.0 reduce-scatter.9
  321.6 37.8 all-gather.13
  377.8 78.4 reduce-scatter.5
where the time goes:
time: 469 us; the launch traced here: 465 us
  waiting for transfers between devices  296 us (63%)
  local copies, waits for them, and re-layouts  59.8 us (13%)
  other arithmetic  54.6 us (12%)
  matrix products  39 us (8%)
  between operations  14.8 us (3%)
    all_gather x2, waiting for transfers between devices, anti_owner(): lax.all_gather(grad_rows, 'ctx', axis=0, tiled=True)  77.9 us
    reduce_scatter x1, waiting for transfers between devices, on_device(): lax.psum_scatter(own_lags.astype(jnp.bfloat16), 'dp', scatter_dimension=2...  72.5 us
    reduce_scatter x1, waiting for transfers between devices, on_device(): lax.psum_scatter(lax.dot_general(gated, cotangent, (((0,), (0,)), ((), ()...  69.5 us
    all_gather x2, waiting for transfers between devices, causal(): piece = lax.all_gather(source, 'ctx', axis=0, tiled=True)  65.1 us
    dot_general x7, matrix products, to_spectra(): jnp.einsum('fb,...bd->...fd', table, blocks.astype(jnp.float32), precisio...  25 us
    mul x4, other arithmetic, spectral_product(): cross = left_imag * right_imag  22 us
    sub x4, other arithmetic, spectral_product(): left_real * right_real - jnp.concatenate([border, cross, border], axis=-2)  15.5 us
    unnamed x61, local copies, waits for them, and re-layouts  10.9 us
  transfers between devices with their start and end apart: 7, of which 7 were waited for; matrix products, arithmetic and copies ran while one was open for 14% of the time, Pallas kernels for 0%

commit v1 on v0

--- a/solution.py
+++ b/solution.py
@@ -76,7 +76,10 @@
 
     def causal(source, padded_filter):
         initial = jnp.zeros((own_blocks + 1, 2 * block, width), jnp.float32)
-        piece = lax.all_gather(source, "ctx", axis=0, tiled=True)
+        size = lax.axis_size("ctx")
+        parts = jnp.stack([source for _ in range(size)])
+        parts = lax.all_to_all(parts, "ctx", split_axis=0, concat_axis=0)
+        piece = jnp.concatenate(parts, axis=0)
         start = jnp.int32(0)
 
         def work(total):

time: 469 us -> 430 us (0.917)
  waiting for transfers between devices: 296 us -> 231 us
  starting transfers between devices: 0.5 us -> 12.7 us
  local copies, waits for them, and re-layouts: 59.8 us -> 70.8 us
    all_gather x2, waiting for transfers between devices: 65.1 us -> 0.02 us  [anti_owner(): lax.all_gather(source, 'ctx', axis=0, tiled=True)]
    all_to_all x0 -> x2, waiting for transfers between devices: none -> 44.8 us  [causal(): parts = lax.all_to_all(parts, 'ctx', split_axis=0, concat_axis=0)]
    all_gather x2, waiting for transfers between devices: 77.9 us -> 38.3 us  [anti_owner(): lax.all_gather(grad_rows, 'ctx', axis=0, tiled=True)]
    all_to_all x0 -> x2, starting transfers between devices: none -> 12 us  [causal(): parts = lax.all_to_all(parts, 'ctx', split_axis=0, concat_axis=0)]
    slice x2, local copies, waits for them, and re-layouts: 7.57 us -> 12.7 us  [spectral_product(): left_imag = left[..., block + 1:, :]]
    unnamed x61 -> x43, local copies, waits for them, and re-layouts: 10.9 us -> 9.86 us
  transfers between devices with their start and end apart: 7 -> 9, of which waited for: 7 -> 6; matrix products, arithmetic and copies ran while one was open for 14% -> 24% of each run, Pallas kernels for 0% -> 0%
where the time goes in v1:
time: 430 us; the launch traced here: 425 us
  waiting for transfers between devices  231 us (54%)
  local copies, waits for them, and re-layouts  70.8 us (16%)
  other arithmetic  55.2 us (13%)
  matrix products  39.1 us (9%)
  between operations  15.9 us (4%)
  starting transfers between devices  12.7 us (3%)
    reduce_scatter x1, waiting for transfers between devices, on_device(): lax.psum_scatter(own_lags.astype(jnp.bfloat16), 'dp', scatter_dimension=2...  72.5 us
    reduce_scatter x1, waiting for transfers between devices, on_device(): lax.psum_scatter(lax.dot_general(gated, cotangent, (((0,), (0,)), ((), ()...  65 us
    all_to_all x2, waiting for transfers between devices, causal(): parts = lax.all_to_all(parts, 'ctx', split_axis=0, concat_axis=0)  44.8 us
    all_gather x2, waiting for transfers between devices, anti_owner(): lax.all_gather(grad_rows, 'ctx', axis=0, tiled=True)  38.3 us
    dot_general x7, matrix products, to_spectra(): jnp.einsum('fb,...bd->...fd', table, blocks.astype(jnp.float32), precisio...  25.4 us
    mul x4, other arithmetic, spectral_product(): cross = left_imag * right_imag  22 us
    sub x4, other arithmetic, spectral_product(): left_real * right_real - jnp.concatenate([border, cross, border], axis=-2)  13.7 us
    slice x2, local copies, waits for them, and re-layouts, spectral_product(): left_imag = left[..., block + 1:, :]  12.7 us
  transfers between devices with their start and end apart: 9, of which 6 were waited for; matrix products, arithmetic and copies ran while one was open for 24% of the time, Pallas kernels for 0%

profile of v1, /device:TPU:2, one launch (start us, length us, event | category | flops | bytes accessed | tf_op | source)
XLA Modules:
  0.0 424.8 jit_solution(5188274380071441472)
XLA Ops:
  10.2 8.5 %all-to-all-start = ((bf16[8,128,512]{2,1,0:T(8,128)(2,1)}), bf16[8,128,512]{2,1,0:T(8,128)(2,1)S(1)}, u32[]{:S(2)}, u32[]{:S(2)}) async-start(bf16[8,128,512]{2,1,0:T(8,128)(2,1)} %stack.34), calls=%async_computation | async-start | bytes 2097152 | tf_op jit(solution)/shard_map/all_to_all | solution.py:81
  18.9 3.9 convolution_bitcast_fusion.2
  22.9 8.0 %concatenate.92 = f32[2,16,256,512]{3,2,1,0:T(8,128)} pad(f32[2,8,256,512]{3,2,1,0:T(8,128)S(1)} %convolution_bitcast_fusion.2, f32[]{:T(128)} %constant.162.clone.1), padding=0_0x8_0x0_0x0_0 | pad | bytes 25165828 | tf_op jit(solution)/shard_map/concatenate | solution.py:71
  33.5 13.9 %all-to-all-done = bf16[8,128,512]{2,1,0:T(8,128)(2,1)S(1)} async-done(((bf16[8,128,512]{2,1,0:T(8,128)(2,1)}), bf16[8,128,512]{2,1,0:T(8,128)(2,1)S(1)}, u32[]{:S(2)}, u32[]{:S(2)}) %all-to-all-start) | async-done | bytes 1048608 | tf_op jit(solution)/shard_map/all_to_all | solution.py:81
  47.4 34.2 %conditional.2 = (f32[2,256,512]{2,1,0:T(8,128)S(1)}) conditional(s32[]{:T(128)} %convert_element_type.91, () %tuple.25, (f32[2,16,256,512]{3,2,1,0:T(8,128)}, s32[]{:T(128)}, bf16[8,128,512]{2,1,0:T(8,128)(2,1)S(1)}, f32[256,128]{1,0:T(8,128)}) %tuple.26), branch_computations={%region_0.1_spmd, %region_1.4_spmd} | conditional | flops 1623326720 | bytes 128827608 | solution.py:104
  47.4 4.4 %slice.174 = f32[1,16,256,512]{3,2,1,0:T(8,128)S(1)} slice(f32[2,16,256,512]{3,2,1,0:T(8,128)} %get-tuple-element.61), slice={[0:1], [0:16], [0:256], [0:512]} | slice | bytes 16777216 | tf_op jit(solution)/shard_map/slice | solution.py:143
  51.8 3.0 dynamic-slice_bitcast_fusion.1
  54.9 6.3 %fusion.87 = (f32[8,127,512]{2,1,0:T(8,128)}, f32[8,127,512]{2,1,0:T(8,128)}, f32[8,127,512]{2,1,0:T(8,128)}, f32[8,127,512]{2,1,0:T(8,128)}) fusion(f32[8,256,512]{2,1,0:T(8,128)} %get-tuple-element.96, f32[8,256,512]{2,1,0:T(8,128)S(1)} %get-tuple-element.97), kind=kLoop, calls=%fused_computation.191 | loop fusion | bytes 16646144 | tf_op jit(solution)/shard_map/cond/branch_1_fun/slice | solution.py:43
  61.2 3.0 convolution_bitcast_fusion
  64.2 7.5 %reverse_multiply_fusion.1 = (f32[8,127,512]{2,1,0:T(8,128)}, f32[8,127,512]{2,1,0:T(8,128)S(1)}, f32[8,127,512]{2,1,0:T(8,128)S(1)}, f32[8,127,512]{2,1,0:T(8,128)}) fusion(f32[8,127,512]{2,1,0:T(8,128)} %get-tuple-element.106, f32[8,256,512]{2,1,0:T(8,128)S(1)} %convolution_bitcast_fusion, f32[8,127,512]{2,1,0:T(8,128)} %get-tuple-element.107, ...), kind=kLoop, calls=%fused_computation.14 | loop fusion | flops 4161536 | bytes 20807680 | tf_op jit(solution)/shard_map/cond/branch_1_fun/mul | solution.py:48
  75.8 2.8 fusion
  85.9 3.6 all-to-all-start.1
  90.4 30.9 %all-to-all-done.1 = bf16[8,128,512]{2,1,0:T(8,128)(2,1)S(1)} async-done(((bf16[8,128,512]{2,1,0:T(8,128)(2,1)}), bf16[8,128,512]{2,1,0:T(8,128)(2,1)S(1)}, u32[]{:S(2)}, u32[]{:S(2)}) %all-to-all-start.1) | async-done | bytes 1048608 | tf_op jit(solution)/shard_map/all_to_all | solution.py:81
  121.4 34.3 %conditional.3 = (f32[2,256,512]{2,1,0:T(8,128)S(1)}) conditional(s32[]{:T(128)} %convert_element_type.91, () %tuple.24, (f32[2,16,256,512]{3,2,1,0:T(8,128)}, s32[]{:T(128)}, bf16[8,128,512]{2,1,0:T(8,128)(2,1)S(1)}, f32[256,128]{1,0:T(8,128)}) %tuple.27), branch_computations={%region_4.5_spmd, %region_5.8_spmd} | conditional | flops 1623326720 | bytes 128827608 | solution.py:104
  121.4 4.4 %slice.190 = f32[1,16,256,512]{3,2,1,0:T(8,128)S(1)} slice(f32[2,16,256,512]{3,2,1,0:T(8,128)} %get-tuple-element.72), slice={[1:2], [0:16], [0:256], [0:512]} | slice | bytes 16777216 | tf_op jit(solution)/shard_map/slice | solution.py:145
  125.8 3.0 dynamic-slice_bitcast_fusion.3
  128.9 6.4 %fusion.89 = (f32[8,127,512]{2,1,0:T(8,128)}, f32[8,127,512]{2,1,0:T(8,128)}, f32[8,127,512]{2,1,0:T(8,128)}, f32[8,127,512]{2,1,0:T(8,128)}) fusion(f32[8,256,512]{2,1,0:T(8,128)} %get-tuple-element.112, f32[8,256,512]{2,1,0:T(8,128)S(1)} %get-tuple-element.113), kind=kLoop, calls=%fused_computation.193 | loop fusion | bytes 16646144 | tf_op jit(solution)/shard_map/cond/branch_1_fun/slice | solution.py:43
  135.3 3.0 convolution_bitcast_fusion.1
  138.2 7.5 %reverse_multiply_fusion.3 = (f32[8,127,512]{2,1,0:T(8,128)}, f32[8,127,512]{2,1,0:T(8,128)S(1)}, f32[8,127,512]{2,1,0:T(8,128)S(1)}, f32[8,127,512]{2,1,0:T(8,128)}) fusion(f32[8,127,512]{2,1,0:T(8,128)} %get-tuple-element.122, f32[8,256,512]{2,1,0:T(8,128)S(1)} %convolution_bitcast_fusion.1, f32[8,127,512]{2,1,0:T(8,128)} %get-tuple-element.123, ...), kind=kLoop, calls=%fused_computation.32 | loop fusion | flops 4161536 | bytes 20807680 | tf_op jit(solution)/shard_map/cond/branch_1_fun/mul | solution.py:48
  161.8 8.2 %slice_bitcast_fusion = (f32[8,256,512]{2,1,0:T(8,128)}, f32[8,256,512]{2,1,0:T(8,128)}) fusion(f32[2,8,256,512]{3,2,1,0:T(8,128)} %copy-done.2), kind=kLoop, calls=%fused_computation.50 | loop fusion | bytes 16777216 | tf_op jit(solution)/shard_map/slice | solution.py:110
  171.5 4.5 %convolution_bitcast_fusion.3 = f32[8,256,512]{2,1,0:T(8,128)} fusion(bf16[8,128,512]{2,1,0:T(8,128)(2,1)S(1)} %bitcast.151, s32[256]{0:T(256)S(1)} %get-tuple-element.95, pred[256]{0:T(512)(128)(4,1)S(1)} %iota_compare_fusion), kind=kOutput, calls=%fused_computation.67 | convolution fusion | flops 1611104256 | bytes 5244160 | tf_op jit(solution)/shard_map/fb,...bd->...fd/dot_general | solution.py:32
  176.0 65.0 %reduce-scatter.8.cloned.1.call-done = bf16[16,512]{1,0:T(8,128)(2,1)} async-done(((bf16[512,512]{1,0:T(8,128)(2,1)}), bf16[16,512]{1,0:T(8,128)(2,1)}) %reduce-scatter.8.cloned.1.call-update) | async-done | bytes 16400 | tf_op jit(solution)/shard_map/reduce_scatter | solution.py:165
  250.8 3.8 fusion.17
  254.6 3.6 fusion.9
  258.3 2.9 maximum_reduce_fusion.4
  263.2 5.7 %convolution_bitcast_fusion.4 = f32[8,256,512]{2,1,0:T(8,128)} fusion(bf16[8,128,512]{2,1,0:T(8,128)(2,1)} %bitcast.156, s32[256]{0:T(256)S(1)} %get-tuple-element.95, pred[256]{0:T(512)(128)(4,1)S(1)} %iota_compare_fusion), kind=kOutput, calls=%fused_computation.68 | convolution fusion | flops 1611104256 | bytes 5244160 | tf_op jit(solution)/shard_map/fb,...bd->...fd/dot_general | solution.py:32
  270.6 8.9 %reduce-scatter.10.cloned.1.call-done = bf16[64,16]{1,0:T(8,128)(2,1)} async-done(((bf16[512,16]{1,0:T(8,128)(2,1)}), bf16[64,16]{1,0:T(8,128)(2,1)}) %reduce-scatter.10.cloned.1.call-update) | async-done | bytes 2064
  281.3 38.3 %all-gather.10.cloned.1.call-done = bf16[1,1024,512]{1,2,0:T(8,128)(2,1)} async-done(((bf16[1,128,512]{1,2,0:T(8,128)(2,1)}), bf16[1,1024,512]{1,2,0:T(8,128)(2,1)}) %all-gather.10.cloned.1.call-update) | async-done | bytes 1048592 | tf_op jit(solution)/shard_map/all_gather | solution.py:113
  327.7 3.1 fusion.16
  330.8 4.4 %fusion.8 = (f32[8,129,512]{2,1,0:T(8,128)S(1)}, f32[8,129,512]{2,1,0:T(8,128)}) fusion(f32[8,1,512]{2,1,0:T(1,128)S(1)} %broadcast.149, f32[8,256,512]{2,1,0:T(8,128)S(1)} %copy-done.3, f32[8,127,512]{2,1,0:T(8,128)S(1)} %get-tuple-element.128, s32[]{:T(128)S(6)} %select_n.74, f32[8,256,512]{2,1,0:T(8,128)S(1)} %multiply_add_fusion.4, ...), kind=kLoop, calls=%fused_computation.61 | loop fusion | flops 4227072 | bytes 16826372 | tf_op jit(solution)/shard_map/while/body/eval_jaxpr/sub | solution.py:50
  338.9 3.0 maximum_reduce_fusion.5
  343.7 72.5 %reduce-scatter.6.cloned.1.call-done = bf16[2,128,16]{1,2,0:T(8,128)(2,1)} async-done(((bf16[2,128,512]{1,2,0:T(8,128)(2,1)}), bf16[2,128,16]{1,2,0:T(8,128)(2,1)}) %reduce-scatter.6.cloned.1.call-update) | async-done | bytes 8208 | tf_op jit(solution)/shard_map/reduce_scatter | solution.py:160
  (118 shorter events, 64.6 us)
Async XLA Ops:
  8.0 10.9 %copy-start = (bf16[2,1024,512]{2,1,0:T(8,128)(2,1)S(1)}, bf16[2,1024,512]{2,1,0:T(8,128)(2,1)}, u32[]{:S(2)}) copy-start(bf16[2,1024,512]{2,1,0:T(8,128)(2,1)} %param.13) | copy-start | bytes 6291460
  8.0 10.7 %copy-start.20 = (bf16[1,128,512]{2,1,0:T(8,128)(2,1)S(1)}, bf16[1,128,512]{2,1,0:T(8,128)(2,1)}, u32[]{:S(2)}) copy-start(bf16[1,128,512]{2,1,0:T(8,128)(2,1)} %param.11) | copy-start | bytes 393220
  10.2 37.2 %all-to-all-start = ((bf16[8,128,512]{2,1,0:T(8,128)(2,1)}), bf16[8,128,512]{2,1,0:T(8,128)(2,1)S(1)}, u32[]{:S(2)}, u32[]{:S(2)}) async-start(bf16[8,128,512]{2,1,0:T(8,128)(2,1)} %stack.34), calls=%async_computation | async-start | bytes 2097152 | tf_op jit(solution)/shard_map/all_to_all | solution.py:81
  18.8 64.2 %copy-start.15 = (bf16[1,128,512]{1,2,0:T(8,128)(2,1)}, bf16[1,128,512]{1,2,0:T(8,128)(2,1)S(1)}, u32[]{:S(2)}) copy-start(bf16[1,128,512]{1,2,0:T(8,128)(2,1)S(1)} %copy.24) | copy-start | bytes 393220
  22.9 8.3 %copy-start.2 = (f32[2,8,256,512]{3,2,1,0:T(8,128)}, f32[2,8,256,512]{3,2,1,0:T(8,128)S(1)}, u32[]{:S(2)}) copy-start(f32[2,8,256,512]{3,2,1,0:T(8,128)S(1)} %convolution_bitcast_fusion.2) | copy-start | bytes 25165828
  73.6 1.6 copy-start.7
  73.6 2.2 copy-start.8
  83.0 7.3 %copy-start.21 = (bf16[1,128,512]{2,1,0:T(8,128)(2,1)S(1)}, bf16[1,128,512]{2,1,0:T(8,128)(2,1)}, u32[]{:S(2)}) copy-start(bf16[1,128,512]{2,1,0:T(8,128)(2,1)} %param.12) | copy-start | bytes 393220
  84.7 4.8 %copy-start.17 = (bf16[1,128,512]{1,2,0:T(8,128)(2,1)}, bf16[1,128,512]{1,2,0:T(8,128)(2,1)S(1)}, u32[]{:S(2)}) copy-start(bf16[1,128,512]{1,2,0:T(8,128)(2,1)S(1)} %get-tuple-element.150) | copy-start | bytes 393220
  85.9 35.4 %all-to-all-start.1 = ((bf16[8,128,512]{2,1,0:T(8,128)(2,1)}), bf16[8,128,512]{2,1,0:T(8,128)(2,1)S(1)}, u32[]{:S(2)}, u32[]{:S(2)}) async-start(bf16[8,128,512]{2,1,0:T(8,128)(2,1)} %stack.36), calls=%async_computation.1 | async-start | bytes 2097152 | tf_op jit(solution)/shard_map/all_to_all | solution.py:81
  89.5 80.5 %all-gather.14.cloned.1.call-start = ((), (), s32[]{:S(2)}) async-start(), calls=%async_computation.10 | async-start | bytes 1179648 | tf_op jit(solution)/shard_map/all_gather | solution.py:112
  90.2 150.8 %reduce-scatter.8.cloned.1.call-start = ((), (), s32[]{:S(2)}) async-start(), calls=%async_computation.7 | async-start | bytes 540672 | tf_op jit(solution)/shard_map/reduce_scatter | solution.py:165
  147.7 1.6 copy-start.9
  147.7 2.2 copy-start.10
  155.7 4.4 %copy-start.13 = (bf16[512,512]{1,0:T(8,128)(2,1)S(1)}, bf16[512,512]{1,0:T(8,128)(2,1)}, u32[]{:S(2)}) copy-start(bf16[512,512]{1,0:T(8,128)(2,1)} %param.14) | copy-start | bytes 1572868
  155.7 4.4 %copy-start.19 = (bf16[1,128,512]{2,1,0:T(8,128)(2,1)S(1)}, bf16[1,128,512]{2,1,0:T(8,128)(2,1)}, u32[]{:S(2)}) copy-start(bf16[1,128,512]{2,1,0:T(8,128)(2,1)} %param.15) | copy-start | bytes 393220
  157.7 12.3 %copy-start.11 = (f32[512,128]{1,0:T(8,128)}, f32[512,128]{1,0:T(8,128)S(1)}, u32[]{:S(2)}) copy-start(f32[512,128]{1,0:T(8,128)S(1)} %convolution_add_fusion) | copy-start | bytes 786436
  159.8 82.8 %all-gather.8.cloned.1.call-start = ((), (), s32[]{:S(2)}) async-start(), calls=%async_computation.5 | async-start | bytes 1179648 | tf_op jit(solution)/shard_map/all_gather | solution.py:113
  161.0 102.2 %all-gather.12.cloned.1.call-start = ((), (), s32[]{:S(2)}) async-start(), calls=%async_computation.9 | async-start | bytes 1179648 | tf_op jit(solution)/shard_map/all_gather | solution.py:112
  161.8 117.7 %reduce-scatter.10.cloned.1.call-start = ((), (), s32[]{:S(2)}) async-start(), calls=%async_computation.11 | async-start | bytes 147456
  242.6 77.0 %all-gather.10.cloned.1.call-start = ((), (), s32[]{:S(2)}) async-start(), calls=%async_computation.8 | async-start | bytes 1179648 | tf_op jit(solution)/shard_map/all_gather | solution.py:113
  247.4 2.2 copy-start.4
  247.4 3.5 copy-start.6
  258.3 2.9 copy-start.16
  258.3 2.9 copy-start.18
  262.9 153.3 %reduce-scatter.6.cloned.1.call-start = ((), (), s32[]{:S(2)}) async-start(), calls=%async_computation.6 | async-start | bytes 270336 | tf_op jit(solution)/shard_map/reduce_scatter | solution.py:160
  263.2 6.4 %copy-start.12 = (f32[512,128]{1,0:T(8,128)S(1)}, f32[512,128]{1,0:T(8,128)}, u32[]{:S(2)}) copy-start(f32[512,128]{1,0:T(8,128)} %copy-done.11) | copy-start | bytes 786436
  263.2 6.4 %copy-start.14 = (bf16[512,512]{1,0:T(8,128)(2,1)S(1)}, bf16[512,512]{1,0:T(8,128)(2,1)}, u32[]{:S(2)}) copy-start(bf16[512,512]{1,0:T(8,128)(2,1)} %param.14) | copy-start | bytes 1572868
  324.3 2.2 copy-start.3
  324.3 3.5 copy-start.5
  338.9 78.6 %copy-start.1 = (bf16[2,1024,512]{2,1,0:T(8,128)(2,1)S(1)}, bf16[2,1024,512]{2,1,0:T(8,128)(2,1)}, u32[]{:S(2)}) copy-start(bf16[2,1024,512]{2,1,0:T(8,128)(2,1)} %param.13) | copy-start | bytes 6291460
Sparse Core Ops, SparseCore 0:
  92.6 46.3 all-gather.13
  162.9 35.6 all-gather.7
  200.4 37.3 all-gather.11
  242.7 36.7 reduce-scatter.9
  281.6 37.9 all-gather.9
Sparse Core Ops, SparseCore 1:
  159.9 81.1 reduce-scatter.7
  337.6 78.5 reduce-scatter.5
